TPU v7x, 512 devices: a whole 4x8x8 slice. The times are simulated.
512 devices in a mesh: region: 8 (over z_hi, core), shard: 64 (over z_lo, x, y).
Axes of the slice: x: 4, y: 8, z: 8 (z_hi: 4, z_lo: 2; z = z_hi * 2 + z_lo), core: 2. Of those that a mesh axis runs over, the one named last changes fastest.
Arguments:
- points: bfloat16 [49152, 8, 128], P(('region', 'shard')), may hold values from -12 to 12
- block_owner: int32 [49152, 1], P(('region', 'shard')), may hold values from 0 to 63; in each aligned block of 96 rows (0 to 95, 96 to 191, ...) at most 3 rows name the same one
- block_node: int32 [49152], P(('region', 'shard')), may hold values from 0 to 1
- queries: bfloat16 [131072, 128], P(('region', 'shard')), may hold values from -240 to 240
- w_in: bfloat16 [128, 768], replicated, may hold values from -0.5 to 0.5
- w_key: bfloat16 [768, 768], replicated, may hold values from -0.21875 to 0.21875
- w_value: bfloat16 [768, 768], replicated, may hold values from -0.21875 to 0.21875
- w_query: bfloat16 [128, 768], replicated, may hold values from -0.5 to 0.5
- w_out: bfloat16 [768, 128], replicated, may hold values from -0.21875 to 0.21875
Outputs:
- readout: bfloat16 [131072, 128], P(('region', 'shard'))
Inputs may be any that keep to these rules, and one draw needn't show every extreme that they name: `block_owner`: among the 96 blocks of one device no shard is named more than 3 times, and some device names one shard exactly 3 times.
All inputs are finite; a program needn't handle non-finite values.
Results may differ from a plain program's by a relative error of at most 0.018.
Values may be sent and summed in bfloat16 or wider, within the bound.
No kernel may reach another device: no remote copies, remote signals or barrier semaphores. Data moves between devices by JAX's collectives and lax.ppermute only.
A program may use at most 64 MiB of HBM per device.

v0:
```python
import math
import jax
import jax.numpy as jnp
from jax import lax
from jax.sharding import PartitionSpec as P

HEADS = 12
HEAD_DIM = 64
S_DEV = 2


def layer_norm(pooled):
    mean = jnp.mean(pooled, axis=-1, keepdims=True)
    centred = pooled - mean
    spread = jnp.mean(centred * centred, axis=-1, keepdims=True)
    return (centred * lax.rsqrt(spread + 1e-05)).astype(jnp.bfloat16)


def block_ranks(owner_shard, shard_count):
    onehot = (owner_shard[..., None] == jnp.arange(shard_count, dtype=jnp.int32)).astype(jnp.int32)
    before = jnp.cumsum(onehot, axis=-2) - onehot
    return jnp.sum(before * onehot, axis=-1)


def body(points, block_owner, block_node, queries, w_in, w_key, w_value, w_query, w_out):
    shard_count = lax.axis_size("shard")
    block_count, block_points, in_features = points.shape
    model_width = w_in.shape[1]
    capacity = max(2, 2 * block_count // shard_count)
    owner_shard = block_owner[:, 0]
    routing = lax.all_gather(
        jnp.stack([owner_shard, block_node], axis=1), "shard", axis=0, tiled=True
    )
    routing = routing.reshape(shard_count, block_count, 2)
    every_owner = routing[:, :, 0]
    every_node = routing[:, :, 1]
    this_shard = lax.axis_index("shard")
    position = jnp.arange(shard_count, dtype=jnp.int32)[:, None] * capacity + block_ranks(
        every_owner, shard_count
    )
    arrives_here = every_owner == this_shard
    node_onehot = (
        (every_node[..., None] == jnp.arange(S_DEV, dtype=jnp.int32)) & arrives_here[..., None]
    ).astype(jnp.float32)
    node_onehot = node_onehot.reshape(shard_count * block_count, S_DEV)
    slot_onehot = (
        position.reshape(-1)[:, None]
        == jnp.arange(shard_count * capacity, dtype=jnp.int32)[None, :]
    ).astype(jnp.float32)
    assign = jnp.dot(node_onehot.T, slot_onehot, precision=lax.Precision.HIGHEST)
    slot_index = owner_shard * capacity + block_ranks(owner_shard, shard_count)
    outgoing = (
        jnp.zeros((shard_count * capacity, block_points, in_features), points.dtype)
        .at[slot_index]
        .set(points)
    )
    outgoing = outgoing.reshape(shard_count, capacity, block_points, in_features)
    messages = jax.nn.gelu(
        jnp.einsum(
            "jkpc,cd->jkpd",
            lax.all_to_all(outgoing, "shard", split_axis=0, concat_axis=0, tiled=True),
            w_in,
            preferred_element_type=jnp.float32,
        )
    ).astype(jnp.bfloat16)
    per_slot = messages.reshape(shard_count * capacity, block_points * model_width)
    pooled = jnp.dot(assign.astype(jnp.bfloat16), per_slot, preferred_element_type=jnp.float32)
    pooled = jnp.sum(pooled.reshape(S_DEV, block_points, model_width), axis=1)
    normed = layer_norm(pooled)
    query_count = queries.shape[0]
    query_vec = jnp.dot(queries, w_query, preferred_element_type=jnp.float32).astype(jnp.bfloat16)
    query_heads = query_vec.reshape(query_count, HEADS, HEAD_DIM)
    score_scale = HEAD_DIM ** (-0.5)
    starting = (
        jnp.full((query_count, HEADS), -1e30, jnp.float32),
        jnp.zeros((query_count, HEADS), jnp.float32),
        jnp.zeros((query_count, HEADS, HEAD_DIM), jnp.float32),
    )
    key_rows = jnp.dot(normed, w_key, preferred_element_type=jnp.float32).astype(jnp.bfloat16)
    value_rows = jnp.dot(normed, w_value, preferred_element_type=jnp.float32).astype(jnp.bfloat16)
    anchor_rows = jnp.concatenate([key_rows, value_rows], axis=1)
    region_rows = lax.all_gather(anchor_rows, "shard", axis=0, tiled=True)
    key_values = lax.all_gather(region_rows, "region", axis=0, tiled=True)
    row_count = key_values.shape[0]
    step_rows = math.gcd(row_count, 256)

    def one_block(block_index, carried):
        peak_now, denominator, numerator = carried
        block_rows = lax.dynamic_slice_in_dim(key_values, block_index * step_rows, step_rows, 0)
        key_block = block_rows[:, :model_width].reshape(step_rows, HEADS, HEAD_DIM)
        value_block = block_rows[:, model_width:].reshape(step_rows, HEADS, HEAD_DIM)
        scores = (
            jnp.einsum("qhd,rhd->qhr", query_heads, key_block, preferred_element_type=jnp.float32)
            * score_scale
        )
        new_peak = jnp.maximum(peak_now, jnp.max(scores, axis=-1))
        rescale = jnp.exp(peak_now - new_peak)
        exponent = jnp.exp(scores - new_peak[..., None])
        denominator = denominator * rescale + jnp.sum(exponent, axis=-1)
        numerator = numerator * rescale[..., None] + jnp.einsum(
            "qhr,rhd->qhd",
            exponent.astype(jnp.bfloat16),
            value_block,
            preferred_element_type=jnp.float32,
        )
        return (new_peak, denominator, numerator)

    finished = lax.fori_loop(0, row_count // step_rows, one_block, starting)
    peak_final, denominator, numerator = finished
    attended = (
        (numerator / denominator[..., None]).astype(jnp.bfloat16).reshape(query_count, model_width)
    )
    return jnp.dot(attended, w_out, preferred_element_type=jnp.float32).astype(jnp.bfloat16)


def solution(mesh):
    return jax.shard_map(
        body,
        mesh=mesh,
        in_specs=(
            P(("region", "shard"), None, None),
            P(("region", "shard"), None),
            P(("region", "shard")),
            P(("region", "shard"), None),
            P(),
            P(),
            P(),
            P(),
            P(),
        ),
        out_specs=P(("region", "shard"), None),
        check_vma=False,
    )
```

profile of v0, /device:TPU:1, one launch (start us, length us, event | category | flops | bytes accessed | tf_op | source)
XLA Modules:
  0.0 421.8 jit_solution(3084942516669463617)
XLA Ops:
  6.5 0.8 fusion.38
  7.5 0.8 select_reduce_fusion
  8.4 0.7 fusion.42
  9.0 0.8 broadcast_in_dim.17
  9.8 10.0 %scatter_fusion = bf16[192,8,128]{2,1,0:T(8,128)(2,1)} fusion(bf16[192,8,128]{2,1,0:T(8,128)(2,1)} %broadcast_in_dim.17, s32[96]{0:T(128)S(1)} %fusion.42, bf16[96,8,128]{2,1,0:T(8,128)(2,1)} %param.11), kind=kCustom, calls=%fused_computation | custom fusion | bytes 590208 | tf_op jit(solution)/shard_map/scatter | solution.py:55
  19.8 12.9 %all-to-all-start = ((bf16[64,3,8,128]{3,2,1,0:T(8,128)(2,1)}), bf16[64,3,8,128]{3,2,1,0:T(8,128)(2,1)S(1)}, u32[]{:S(2)}, u32[]{:S(2)}) async-start(bf16[64,3,8,128]{3,2,1,0:T(8,128)(2,1)} %bitcast.7), calls=%async_computation | async-start | bytes 786432 | tf_op jit(solution)/shard_map/all_to_all | solution.py:61
  32.8 0.7 add_bitcast_fusion
  33.5 129.2 %all-gather = s32[64,96,2]{1,2,0:T(2,128)S(1)} all-gather(s32[1,96,2]{1,2,0:T(2,128)S(1)} %add_bitcast_fusion), channel_id=1, replica_groups=mesh['region'=8,'shard'=64] {'shard'}, dimensions={0}, use_global_device_ids=true | all-gather | bytes 49920 | tf_op jit(solution)/shard_map/all_gather | solution.py:31
  163.2 3.3 fusion.27
  166.8 0.8 fusion.34
  167.6 1.6 fusion.22
  170.9 124.8 %all-gather.1 = bf16[64,2,1536]{2,1,0:T(2,128)(2,1)S(1)} all-gather(bf16[1,2,1536]{2,1,0:T(2,128)(2,1)S(1)} %maximum_bitcast_fusion), channel_id=1, replica_groups=mesh['region'=8,'shard'=64] {'shard'}, dimensions={0}, use_global_device_ids=true | all-gather | bytes 399360 | tf_op jit(solution)/shard_map/all_gather | solution.py:82
  295.9 0.9 copy.46
  297.3 103.9 %all-gather.4.cloned.1.call-done = bf16[1024,1536]{0,1:T(8,128)(2,1)} async-done(((bf16[128,1536]{0,1:T(8,128)(2,1)}), bf16[1024,1536]{0,1:T(8,128)(2,1)}) %all-gather.4.cloned.1.call-update) | async-done | bytes 3145744 | tf_op jit(solution)/shard_map/all_gather | solution.py:83
  401.1 12.8 %while.18 = (s32[]{:T(128)}, f32[256,12]{0,1:T(8,128)S(1)}, f32[256,12]{0,1:T(8,128)S(1)}, f32[256,12,64]{0,2,1:T(8,128)S(1)}, bf16[1024,1536]{0,1:T(8,128)(2,1)...) while((s32[]{:T(128)}, f32[256,12]{0,1:T(8,128)S(1)}, ...), condition=%wide.region_11.12_spmd.clone, body=%wide.region_8.11_spmd.clone.sunk | while | flops 208223232 | bytes 13959363 | solution.py:108
  401.1 1.2 fusion.68
  403.6 0.8 fusion.71
  404.3 1.2 fusion.68
  406.7 0.8 fusion.71
  407.5 1.2 fusion.68
  409.9 0.8 fusion.71
  410.7 1.2 fusion.68
  413.1 0.8 fusion.71
  414.0 0.9 convolution_convert_fusion.1
  (59 shorter events, 7.9 us)
Async XLA Ops:
  6.5 163.6 %copy-start = (bf16[768,768]{1,0:T(8,128)(2,1)S(1)}, bf16[768,768]{1,0:T(8,128)(2,1)}, u32[]{:S(2)}) copy-start(bf16[768,768]{1,0:T(8,128)(2,1)} %param.17) | copy-start | bytes 3538948
  6.5 161.1 %copy-start.5 = (bf16[128,768]{1,0:T(8,128)(2,1)S(1)}, bf16[128,768]{1,0:T(8,128)(2,1)}, u32[]{:S(2)}) copy-start(bf16[128,768]{1,0:T(8,128)(2,1)} %param.15) | copy-start | bytes 589828
  19.8 147.8 %all-to-all-start = ((bf16[64,3,8,128]{3,2,1,0:T(8,128)(2,1)}), bf16[64,3,8,128]{3,2,1,0:T(8,128)(2,1)S(1)}, u32[]{:S(2)}, u32[]{:S(2)}) async-start(bf16[64,3,8,128]{3,2,1,0:T(8,128)(2,1)} %bitcast.7), calls=%async_computation | async-start | bytes 786432 | tf_op jit(solution)/shard_map/all_to_all | solution.py:61
  32.8 368.4 %all-gather.4.cloned.1.call-start = ((), (), s32[]{:S(2)}) async-start(), calls=%async_computation.1 | async-start | bytes 3538944 | tf_op jit(solution)/shard_map/all_gather | solution.py:83
  169.3 1.3 copy-start.4
  169.9 126.9 %copy-start.1 = (bf16[128,768]{1,0:T(8,128)(2,1)S(1)}, bf16[128,768]{1,0:T(8,128)(2,1)}, u32[]{:S(2)}) copy-start(bf16[128,768]{1,0:T(8,128)(2,1)} %param.18) | copy-start | bytes 589828
  170.0 126.9 %copy-start.3 = (bf16[256,128]{1,0:T(8,128)(2,1)S(1)}, bf16[256,128]{1,0:T(8,128)(2,1)}, u32[]{:S(2)}) copy-start(bf16[256,128]{1,0:T(8,128)(2,1)} %param.14) | copy-start | bytes 196612
  401.1 12.8 %copy-start.2 = (bf16[768,128]{1,0:T(8,128)(2,1)S(1)}, bf16[768,128]{1,0:T(8,128)(2,1)}, u32[]{:S(2)}) copy-start(bf16[768,128]{1,0:T(8,128)(2,1)} %param.19) | copy-start | bytes 589828
Sparse Core Ops, SparseCore 0:
  296.9 104.1 all-gather.3
where the time goes:
time: 423 us; the launch traced here: 422 us
  blocking collectives  254 us (60%)
  waiting for transfers between devices  104 us (25%)
  local copies, waits for them, and re-layouts  17.4 us (4%)
  between operations  13.6 us (3%)
  starting transfers between devices  13 us (3%)
  matrix products  10.4 us (2%)
  other arithmetic  9.21 us (2%)
    all_gather x1, blocking collectives, body(): lax.all_gather(jnp.stack([owner_shard, block_node], axis=1), 'shard', axi...  129 us
    all_gather x1, blocking collectives, body(): region_rows = lax.all_gather(anchor_rows, 'shard', axis=0, tiled=True)  125 us
    all_gather x1, waiting for transfers between devices, body(): key_values = lax.all_gather(region_rows, 'region', axis=0, tiled=True)  104 us
    all_to_all x1, starting transfers between devices, body(): lax.all_to_all(outgoing, 'shard', split_axis=0, concat_axis=0, tiled=True)  12.9 us
    scatter x1, local copies, waits for them, and re-layouts, body(): outgoing = jnp.zeros((shard_count * capacity, block_points, in_features),...  10 us
  transfers between devices with their start and end apart: 2, of which 1 were waited for; matrix products, arithmetic and copies ran while one was open for 1% of the time, Pallas kernels for 0%

commit v1 on v0

--- a/solution.py
+++ b/solution.py
@@ -28,8 +28,16 @@
     model_width = w_in.shape[1]
     capacity = max(2, 2 * block_count // shard_count)
     owner_shard = block_owner[:, 0]
-    routing = lax.all_gather(
-        jnp.stack([owner_shard, block_node], axis=1), "shard", axis=0, tiled=True
+    routing = jnp.concatenate(
+        lax.all_to_all(
+            jnp.stack(
+                lax.psum(1, "shard") * [jnp.stack([owner_shard, block_node], axis=1)], axis=0
+            ),
+            "shard",
+            0,
+            0,
+        ),
+        axis=0,
     )
     routing = routing.reshape(shard_count, block_count, 2)
     every_owner = routing[:, :, 0]

time: 423 us -> 290 us (0.69)
  blocking collectives: 254 us -> 128 us
  waiting for transfers between devices: 104 us -> 86 us
  starting transfers between devices: 13 us -> 23.7 us
    all_gather x1 -> x0, blocking collectives: 129 us -> none  [body(): lax.all_gather(jnp.stack([owner_shard, block_node], axis=1), 'shard', axi...]
    all_gather x1, waiting for transfers between devices: 104 us -> 77.3 us  [body(): key_values = lax.all_gather(region_rows, 'region', axis=0, tiled=True)]
    all_to_all x0 -> x1, starting transfers between devices: none -> 12.9 us  [body(): lax.all_to_all(jnp.stack(lax.psum(1, 'shard') * [jnp.stack([owner_shard,...]
    all_to_all x1, waiting for transfers between devices: 0.01 us -> 8.69 us  [body(): lax.all_to_all(outgoing, 'shard', split_axis=0, concat_axis=0, tiled=True)]
  transfers between devices with their start and end apart: 2 -> 3, of which waited for: 1 -> 2; matrix products, arithmetic and copies ran while one was open for 1% -> 6% of each run, Pallas kernels for 0% -> 0%
where the time goes in v1:
time: 290 us; the launch traced here: 289 us
  blocking collectives  128 us (44%)
  waiting for transfers between devices  86 us (30%)
  starting transfers between devices  23.7 us (8%)
  local copies, waits for them, and re-layouts  18 us (6%)
  between operations  13.6 us (5%)
  matrix products  10.5 us (4%)
  other arithmetic  9.21 us (3%)
    all_gather x1, blocking collectives, body(): region_rows = lax.all_gather(anchor_rows, 'shard', axis=0, tiled=True)  128 us
    all_gather x1, waiting for transfers between devices, body(): key_values = lax.all_gather(region_rows, 'region', axis=0, tiled=True)  77.3 us
    all_to_all x1, starting transfers between devices, body(): lax.all_to_all(jnp.stack(lax.psum(1, 'shard') * [jnp.stack([owner_shard,...  12.9 us
    all_to_all x1, starting transfers between devices, body(): lax.all_to_all(outgoing, 'shard', split_axis=0, concat_axis=0, tiled=True)  10.8 us
    scatter x1, local copies, waits for them, and re-layouts, body(): outgoing = jnp.zeros((shard_count * capacity, block_points, in_features),...  10 us
    all_to_all x1, waiting for transfers between devices, body(): lax.all_to_all(outgoing, 'shard', split_axis=0, concat_axis=0, tiled=True)  8.69 us
  transfers between devices with their start and end apart: 3, of which 2 were waited for; matrix products, arithmetic and copies ran while one was open for 6% of the time, Pallas kernels for 0%

profile of v1, /device:TPU:1, one launch (start us, length us, event | category | flops | bytes accessed | tf_op | source)
XLA Modules:
  0.0 288.9 jit_solution(15293240421452261000)
XLA Ops:
  6.5 0.8 pad_add_fusion
  8.0 12.9 %all-to-all-start = ((s32[64,96,2]{1,2,0:T(2,128)}), s32[64,96,2]{1,2,0:T(2,128)S(1)}, u32[]{:S(2)}, u32[]{:S(2)}) async-start(s32[64,96,2]{1,2,0:T(2,128)} %stack.8), calls=%async_computation | async-start | bytes 131072 | tf_op jit(solution)/shard_map/all_to_all | solution.py:32
  20.9 0.7 fusion.38
  21.8 0.8 select_reduce_fusion
  23.3 0.8 broadcast_in_dim.17
  24.1 10.0 %scatter_fusion = bf16[192,8,128]{2,1,0:T(8,128)(2,1)} fusion(bf16[192,8,128]{2,1,0:T(8,128)(2,1)} %broadcast_in_dim.17, s32[96]{0:T(128)S(1)} %fusion.42, bf16[96,8,128]{2,1,0:T(8,128)(2,1)} %param.11), kind=kCustom, calls=%fused_computation | custom fusion | bytes 590208 | tf_op jit(solution)/shard_map/scatter | solution.py:63
  34.1 10.8 %all-to-all-start.1 = ((bf16[64,3,8,128]{3,2,1,0:T(8,128)(2,1)}), bf16[64,3,8,128]{3,2,1,0:T(8,128)(2,1)S(1)}, u32[]{:S(2)}, u32[]{:S(2)}) async-start(bf16[64,3,8,128]{3,2,1,0:T(8,128)(2,1)} %bitcast.6), calls=%async_computation.1 | async-start | bytes 786432 | tf_op jit(solution)/shard_map/all_to_all | solution.py:69
  45.4 3.3 %fusion.27 = s32[64,96]{0,1:T(8,128)S(1)} fusion(s32[64,96]{0,1:T(8,128)S(1)} %copy.42), kind=kOutput, calls=%fused_computation.33 | output fusion | flops 40101888 | bytes 49152 | tf_op jit(solution)/shard_map/jit(cumsum)/reduce_window_sum | solution.py:21
  49.0 0.8 fusion.34
  49.8 8.7 %all-to-all-done.1 = bf16[64,3,8,128]{3,2,1,0:T(8,128)(2,1)S(1)} async-done(((bf16[64,3,8,128]{3,2,1,0:T(8,128)(2,1)}), bf16[64,3,8,128]{3,2,1,0:T(8,128)(2,1)S(1)}, u32[]{:S(2)}, u32[]{:S(2)}) %all-to-all-start.1) | async-done | bytes 393248 | tf_op jit(solution)/shard_map/all_to_all | solution.py:69
  58.5 1.6 fusion.22
  61.8 127.5 %all-gather = bf16[64,2,1536]{2,1,0:T(2,128)(2,1)S(1)} all-gather(bf16[1,2,1536]{2,1,0:T(2,128)(2,1)S(1)} %maximum_bitcast_fusion), channel_id=1, replica_groups=mesh['region'=8,'shard'=64] {'shard'}, dimensions={0}, use_global_device_ids=true | all-gather | bytes 399360 | tf_op jit(solution)/shard_map/all_gather | solution.py:90
  189.5 0.9 copy.45
  190.9 77.3 %all-gather.3.cloned.1.call-done = bf16[1024,1536]{0,1:T(8,128)(2,1)} async-done(((bf16[128,1536]{0,1:T(8,128)(2,1)}), bf16[1024,1536]{0,1:T(8,128)(2,1)}) %all-gather.3.cloned.1.call-update) | async-done | bytes 3145744 | tf_op jit(solution)/shard_map/all_gather | solution.py:91
  268.2 12.8 %while.18 = (s32[]{:T(128)}, f32[256,12]{0,1:T(8,128)S(1)}, f32[256,12]{0,1:T(8,128)S(1)}, f32[256,12,64]{0,2,1:T(8,128)S(1)}, bf16[1024,1536]{0,1:T(8,128)(2,1)...) while((s32[]{:T(128)}, f32[256,12]{0,1:T(8,128)S(1)}, ...), condition=%wide.region_11.12_spmd.clone, body=%wide.region_8.11_spmd.clone.sunk | while | flops 208223232 | bytes 13959363 | solution.py:116
  268.2 1.2 fusion.68
  270.7 0.8 fusion.71
  271.5 1.2 fusion.68
  273.8 0.8 fusion.71
  274.6 1.2 fusion.68
  277.0 0.8 fusion.71
  277.8 1.2 fusion.68
  280.2 0.8 fusion.71
  281.1 0.9 convolution_convert_fusion.1
  (61 shorter events, 9.2 us)
Async XLA Ops:
  6.5 54.6 %copy-start = (bf16[768,768]{1,0:T(8,128)(2,1)S(1)}, bf16[768,768]{1,0:T(8,128)(2,1)}, u32[]{:S(2)}) copy-start(bf16[768,768]{1,0:T(8,128)(2,1)} %param.17) | copy-start | bytes 3538948
  6.5 52.0 %copy-start.5 = (bf16[128,768]{1,0:T(8,128)(2,1)S(1)}, bf16[128,768]{1,0:T(8,128)(2,1)}, u32[]{:S(2)}) copy-start(bf16[128,768]{1,0:T(8,128)(2,1)} %param.15) | copy-start | bytes 589828
  8.0 26.1 %all-to-all-start = ((s32[64,96,2]{1,2,0:T(2,128)}), s32[64,96,2]{1,2,0:T(2,128)S(1)}, u32[]{:S(2)}, u32[]{:S(2)}) async-start(s32[64,96,2]{1,2,0:T(2,128)} %stack.8), calls=%async_computation | async-start | bytes 131072 | tf_op jit(solution)/shard_map/all_to_all | solution.py:32
  34.1 24.4 %all-to-all-start.1 = ((bf16[64,3,8,128]{3,2,1,0:T(8,128)(2,1)}), bf16[64,3,8,128]{3,2,1,0:T(8,128)(2,1)S(1)}, u32[]{:S(2)}, u32[]{:S(2)}) async-start(bf16[64,3,8,128]{3,2,1,0:T(8,128)(2,1)} %bitcast.6), calls=%async_computation.1 | async-start | bytes 786432 | tf_op jit(solution)/shard_map/all_to_all | solution.py:69
  44.9 223.4 %all-gather.3.cloned.1.call-start = ((), (), s32[]{:S(2)}) async-start(), calls=%async_computation.2 | async-start | bytes 3538944 | tf_op jit(solution)/shard_map/all_gather | solution.py:91
  60.2 1.3 copy-start.4
  60.9 129.6 %copy-start.1 = (bf16[128,768]{1,0:T(8,128)(2,1)S(1)}, bf16[128,768]{1,0:T(8,128)(2,1)}, u32[]{:S(2)}) copy-start(bf16[128,768]{1,0:T(8,128)(2,1)} %param.18) | copy-start | bytes 589828
  60.9 129.6 %copy-start.3 = (bf16[256,128]{1,0:T(8,128)(2,1)S(1)}, bf16[256,128]{1,0:T(8,128)(2,1)}, u32[]{:S(2)}) copy-start(bf16[256,128]{1,0:T(8,128)(2,1)} %param.14) | copy-start | bytes 196612
  268.2 12.9 %copy-start.2 = (bf16[768,128]{1,0:T(8,128)(2,1)S(1)}, bf16[768,128]{1,0:T(8,128)(2,1)}, u32[]{:S(2)}) copy-start(bf16[768,128]{1,0:T(8,128)(2,1)} %param.19) | copy-start | bytes 589828
Sparse Core Ops, SparseCore 0:
  190.5 77.6 all-gather.2
